TPU v7x, 256 devices: a whole 4x4x8 slice. The times are simulated.
256 devices in a mesh: sx: 8 (over z_hi, x), sy: 4 (over z_lo), af: 8 (over y, core).
Axes of the slice: x: 4, y: 4, z: 8 (z_hi: 2, z_lo: 4; z = z_hi * 4 + z_lo), core: 2. Of those that a mesh axis runs over, the one named last changes fastest.
Arguments:
- volume: bfloat16 [8, 48, 48, 48, 128], P('af', 'sx', 'sy'), may hold values from -6 to 6
- kernel: bfloat16 [3, 3, 3, 128, 256], P(None, None, None, 'sx', ('sy', 'af')), may hold values from -0.109375 to 0.109375
- cotangent: bfloat16 [8, 256, 24, 576], P('sx', ('sy', 'af')), may hold values from -6 to 6
Outputs:
- features: bfloat16 [8, 256, 24, 576], P('sx', ('sy', 'af'))
- volume_grad: bfloat16 [8, 48, 48, 48, 128], P('af', 'sx', 'sy')
- kernel_grad: float32 [3, 3, 3, 128, 256], P(None, None, None, 'sx', ('sy', 'af'))
All inputs are finite; a program needn't handle non-finite values.
Results may differ from a plain program's by a relative error of at most 0.0025.
Values may be sent and summed in bfloat16 or wider, within the bound.
A program may use at most 64 MiB of HBM per device.

v0:
```python
import jax
import jax.numpy as jnp
from jax import lax
from jax.sharding import PartitionSpec as P


def from_behind(value, axis, steps):
    count = lax.axis_size(axis)
    leading, last = (max(0, -steps), min(count, count - steps))
    return lax.ppermute(value, axis, [(source, source + steps) for source in range(leading, last)])


def strided_patch(extended, tap_d, tap_h, tap_w, depth, height, width):
    return extended[
        :,
        tap_d : tap_d + 2 * depth : 2,
        tap_h : tap_h + 2 * height : 2,
        tap_w : tap_w + 2 * width : 2,
        :,
    ]


def weave(even_part, odd_part, axis):
    stacked = jnp.stack([even_part, odd_part], axis=axis + 1)
    shape = list(even_part.shape)
    shape[axis] = shape[axis] * 2
    return stacked.reshape(shape)


def spread_back(grad_space, kernel_full):
    samples, depth, height, width, filters = grad_space.shape
    channels = kernel_full.shape[3]
    grad_flat = grad_space.reshape(-1, filters)
    classes = {}
    for tap_d in range(3):
        for tap_h in range(3):
            for tap_w in range(3):
                term = lax.dot_general(
                    grad_flat,
                    kernel_full[tap_d, tap_h, tap_w],
                    (((1,), (1,)), ((), ())),
                    preferred_element_type=jnp.float32,
                )
                term = term.reshape(samples, depth, height, width, channels)
                pads = [(0, 0)]
                for tap in (tap_d, tap_h, tap_w):
                    pads.append((1, 0) if tap == 2 else (0, 1))
                pads.append((0, 0))
                term = jnp.pad(term, pads)
                key_name = (tap_d % 2, tap_h % 2, tap_w % 2)
                classes[key_name] = classes[key_name] + term if key_name in classes else term
    planes = []
    for parity_d in range(2):
        rows_h = []
        for parity_h in range(2):
            rows_h.append(weave(classes[parity_d, parity_h, 0], classes[parity_d, parity_h, 1], 3))
        planes.append(weave(rows_h[0], rows_h[1], 2))
    whole = weave(planes[0], planes[1], 1)
    return whole[:, : 2 * depth + 1, : 2 * height + 1, : 2 * width + 1, :]


def on_device(volume, kernel, cotangent):
    samples = volume.shape[0]
    depth = volume.shape[1] // 2
    height = volume.shape[2] // 2
    width = volume.shape[3] // 2
    n_sy = lax.axis_size("sy")
    n_af = lax.axis_size("af")
    kernel_part = lax.all_gather(kernel, ("sy", "af"), axis=4, tiled=True)
    kernel_full = lax.all_gather(kernel_part, "sx", axis=3, tiled=True)
    filters = kernel_full.shape[4]
    per_dev = filters // (n_sy * n_af)
    below = from_behind(volume[:, -1:], "sx", 1)
    extended = jnp.concatenate([below, volume], axis=1)
    beside = from_behind(extended[:, :, -1:], "sy", 1)
    extended = jnp.concatenate([beside, extended], axis=2)
    extended = jnp.pad(extended, ((0, 0), (0, 0), (0, 0), (1, 0), (0, 0)))
    rows = samples * depth * height * width
    total = jnp.zeros((rows, filters), jnp.float32)
    for tap_d in range(3):
        for tap_h in range(3):
            for tap_w in range(3):
                patch = strided_patch(extended, tap_d, tap_h, tap_w, depth, height, width).reshape(
                    rows, -1
                )
                total = total + jnp.dot(
                    patch, kernel_full[tap_d, tap_h, tap_w], preferred_element_type=jnp.float32
                )
    conv_space = total.astype(jnp.bfloat16).reshape(
        samples, depth, height, width, n_sy, n_af, per_dev
    )
    by_sample = lax.all_to_all(conv_space, "af", split_axis=5, concat_axis=0, tiled=True)
    gathered = lax.all_to_all(
        lax.all_to_all(by_sample, "sx", split_axis=0, concat_axis=1, tiled=True),
        "sy",
        split_axis=4,
        concat_axis=2,
        tiled=True,
    )
    own_samples = gathered.shape[0]
    edge_d = gathered.shape[1]
    edge_h = gathered.shape[2]
    features = (
        gathered.reshape(own_samples, edge_d, edge_h, width, per_dev)
        .transpose(0, 4, 1, 2, 3)
        .reshape(own_samples, per_dev, edge_d, edge_h * width)
    )
    grad_after = (
        cotangent.reshape(own_samples, per_dev, edge_d, edge_h, width)
        .transpose(0, 2, 3, 4, 1)
        .reshape(own_samples, edge_d, edge_h, width, 1, 1, per_dev)
    )
    grad_region = lax.all_to_all(
        lax.all_to_all(grad_after, "sx", split_axis=1, concat_axis=0, tiled=True),
        "sy",
        split_axis=2,
        concat_axis=4,
        tiled=True,
    )
    grad_back = lax.all_to_all(grad_region, "af", split_axis=0, concat_axis=5, tiled=True)
    grad_space = grad_back.reshape(samples, depth, height, width, filters)
    grad_flat = grad_space.reshape(rows, filters)
    tap_grads = []
    for tap_d in range(3):
        for tap_h in range(3):
            for tap_w in range(3):
                patch = strided_patch(extended, tap_d, tap_h, tap_w, depth, height, width).reshape(
                    rows, -1
                )
                tap_grads.append(
                    lax.dot_general(
                        patch,
                        grad_flat,
                        (((0,), (0,)), ((), ())),
                        preferred_element_type=jnp.float32,
                    )
                )
    kernel_terms = jnp.stack(tap_grads, axis=0).reshape(3, 3, 3, kernel_full.shape[3], filters)
    reduced = lax.psum_scatter(kernel_terms, ("sy", "af"), scatter_dimension=4, tiled=True)
    kernel_grad = lax.psum_scatter(reduced, "sx", scatter_dimension=3, tiled=True)
    partial_grad = spread_back(grad_space, kernel_full)
    from_above = from_behind(partial_grad[:, 0:1], "sx", -1)
    own_depth = partial_grad[:, 1:]
    own_depth = jnp.concatenate([own_depth[:, :-1], own_depth[:, -1:] + from_above], axis=1)
    from_right = from_behind(own_depth[:, :, 0:1].astype(jnp.bfloat16), "sy", -1).astype(
        jnp.float32
    )
    own_height = own_depth[:, :, 1:]
    own_height = jnp.concatenate(
        [own_height[:, :, :-1], own_height[:, :, -1:] + from_right], axis=2
    )
    volume_grad = own_height[:, :, :, 1:]
    return (features, volume_grad.astype(jnp.bfloat16), kernel_grad)


def solution(mesh):
    return jax.shard_map(
        on_device,
        mesh=mesh,
        in_specs=(
            P("af", "sx", "sy", None, None),
            P(None, None, None, "sx", ("sy", "af")),
            P("sx", ("sy", "af"), None, None),
        ),
        out_specs=(
            P("sx", ("sy", "af"), None, None),
            P("af", "sx", "sy", None, None),
            P(None, None, None, "sx", ("sy", "af")),
        ),
        check_vma=False,
    )
```

profile of v0, /device:TPU:8, one launch (start us, length us, event | category | flops | bytes accessed | tf_op | source)
XLA Modules:
  0.0 482.0 jit_solution(499693870692736997)
XLA Ops:
  13.1 10.9 %all-to-all-start.3 = ((bf16[8,2,6912]{2,1,0:T(2,128)(2,1)}), bf16[8,2,6912]{2,1,0:T(2,128)(2,1)S(1)}, u32[]{:S(2)}, u32[]{:S(2)}) async-start(bf16[8,2,6912]{2,1,0:T(2,128)(2,1)} %reshape.377), calls=%async_computation.3 | async-start | bytes 442368 | tf_op jit(solution)/shard_map/all_to_all | solution.py:114
  28.9 6.1 %all-to-all-done.3 = bf16[8,2,6912]{2,1,0:T(2,128)(2,1)S(1)} async-done(((bf16[8,2,6912]{2,1,0:T(2,128)(2,1)}), bf16[8,2,6912]{2,1,0:T(2,128)(2,1)S(1)}, u32[]{:S(2)}, u32[]{:S(2)}) %all-to-all-start.3) | async-done | bytes 221216 | tf_op jit(solution)/shard_map/all_to_all | solution.py:114
  59.7 42.8 %all_gather.6 = bf16[3,3,3,16,256]{3,4,2,1,0:T(8,128)(2,1)S(1)} all-gather(bf16[3,3,3,16,8]{3,4,2,1,0:T(8,128)(2,1)S(1)} %copy-done.50), channel_id=1, replica_groups=mesh['sx'=8,'sy'=4,'af'=8] {'sy','af'}, dimensions={4}, use_global_device_ids=true | all-gather | bytes 228096 | tf_op jit(solution)/shard_map/all_gather | solution.py:69
  104.5 5.5 %slice.257 = bf16[1,3,6,24,128]{4,3,2,1,0:T(8,128)(2,1)} slice(bf16[1,7,13,49,128]{4,3,2,1,0:T(8,128)(2,1)S(1)} %fusion.3), slice={[0:1:1], [0:6:2], [0:12:2], [0:48:2], [0:128:1]} | slice | bytes 221184 | tf_op jit(solution)/shard_map/slice | solution.py:14
  112.1 5.5 %slice.267 = bf16[1,3,6,24,128]{4,3,2,1,0:T(8,128)(2,1)} slice(bf16[1,7,13,49,128]{4,3,2,1,0:T(8,128)(2,1)S(1)} %fusion.3), slice={[0:1:1], [0:6:2], [1:13:2], [2:49:2], [0:128:1]} | slice | bytes 221184 | tf_op jit(solution)/shard_map/slice | solution.py:14
  117.6 5.5 %slice.269 = bf16[1,3,6,24,128]{4,3,2,1,0:T(8,128)(2,1)} slice(bf16[1,7,13,49,128]{4,3,2,1,0:T(8,128)(2,1)S(1)} %fusion.3), slice={[0:1:1], [0:6:2], [2:13:2], [0:48:2], [0:128:1]} | slice | bytes 221184 | tf_op jit(solution)/shard_map/slice | solution.py:14
  123.1 5.5 %slice.271 = bf16[1,3,6,24,128]{4,3,2,1,0:T(8,128)(2,1)} slice(bf16[1,7,13,49,128]{4,3,2,1,0:T(8,128)(2,1)S(1)} %fusion.3), slice={[0:1:1], [0:6:2], [2:13:2], [1:49:2], [0:128:1]} | slice | bytes 221184 | tf_op jit(solution)/shard_map/slice | solution.py:14
  128.6 5.5 %slice.273 = bf16[1,3,6,24,128]{4,3,2,1,0:T(8,128)(2,1)} slice(bf16[1,7,13,49,128]{4,3,2,1,0:T(8,128)(2,1)S(1)} %fusion.3), slice={[0:1:1], [0:6:2], [2:13:2], [2:49:2], [0:128:1]} | slice | bytes 221184 | tf_op jit(solution)/shard_map/slice | solution.py:14
  134.1 5.5 %slice.275 = bf16[1,3,6,24,128]{4,3,2,1,0:T(8,128)(2,1)} slice(bf16[1,7,13,49,128]{4,3,2,1,0:T(8,128)(2,1)S(1)} %fusion.3), slice={[0:1:1], [1:7:2], [0:12:2], [0:48:2], [0:128:1]} | slice | bytes 221184 | tf_op jit(solution)/shard_map/slice | solution.py:14
  145.0 5.5 %slice.279 = bf16[1,3,6,24,128]{4,3,2,1,0:T(8,128)(2,1)} slice(bf16[1,7,13,49,128]{4,3,2,1,0:T(8,128)(2,1)S(1)} %fusion.3), slice={[0:1:1], [1:7:2], [0:12:2], [2:49:2], [0:128:1]} | slice | bytes 221184 | tf_op jit(solution)/shard_map/slice | solution.py:14
  161.4 5.5 %slice.285 = bf16[1,3,6,24,128]{4,3,2,1,0:T(8,128)(2,1)} slice(bf16[1,7,13,49,128]{4,3,2,1,0:T(8,128)(2,1)S(1)} %fusion.3), slice={[0:1:1], [1:7:2], [1:13:2], [2:49:2], [0:128:1]} | slice | bytes 221184 | tf_op jit(solution)/shard_map/slice | solution.py:14
  166.9 5.5 %slice.287 = bf16[1,3,6,24,128]{4,3,2,1,0:T(8,128)(2,1)} slice(bf16[1,7,13,49,128]{4,3,2,1,0:T(8,128)(2,1)S(1)} %fusion.3), slice={[0:1:1], [1:7:2], [2:13:2], [0:48:2], [0:128:1]} | slice | bytes 221184 | tf_op jit(solution)/shard_map/slice | solution.py:14
  172.4 5.5 %slice.289 = bf16[1,3,6,24,128]{4,3,2,1,0:T(8,128)(2,1)} slice(bf16[1,7,13,49,128]{4,3,2,1,0:T(8,128)(2,1)S(1)} %fusion.3), slice={[0:1:1], [1:7:2], [2:13:2], [1:49:2], [0:128:1]} | slice | bytes 221184 | tf_op jit(solution)/shard_map/slice | solution.py:14
  177.9 5.6 %slice.291 = bf16[1,3,6,24,128]{4,3,2,1,0:T(8,128)(2,1)} slice(bf16[1,7,13,49,128]{4,3,2,1,0:T(8,128)(2,1)S(1)} %fusion.3), slice={[0:1:1], [1:7:2], [2:13:2], [2:49:2], [0:128:1]} | slice | bytes 221184 | tf_op jit(solution)/shard_map/slice | solution.py:14
  183.5 5.5 %slice.293 = bf16[1,3,6,24,128]{4,3,2,1,0:T(8,128)(2,1)} slice(bf16[1,7,13,49,128]{4,3,2,1,0:T(8,128)(2,1)S(1)} %fusion.3), slice={[0:1:1], [2:7:2], [0:12:2], [0:48:2], [0:128:1]} | slice | bytes 221184 | tf_op jit(solution)/shard_map/slice | solution.py:14
  196.0 5.5 %slice.303 = bf16[1,3,6,24,128]{4,3,2,1,0:T(8,128)(2,1)} slice(bf16[1,7,13,49,128]{4,3,2,1,0:T(8,128)(2,1)S(1)} %fusion.3), slice={[0:1:1], [2:7:2], [1:13:2], [2:49:2], [0:128:1]} | slice | bytes 221184 | tf_op jit(solution)/shard_map/slice | solution.py:14
  201.5 5.5 %slice.305 = bf16[1,3,6,24,128]{4,3,2,1,0:T(8,128)(2,1)} slice(bf16[1,7,13,49,128]{4,3,2,1,0:T(8,128)(2,1)S(1)} %fusion.3), slice={[0:1:1], [2:7:2], [2:13:2], [0:48:2], [0:128:1]} | slice | bytes 221184 | tf_op jit(solution)/shard_map/slice | solution.py:14
  207.0 5.5 %slice.307 = bf16[1,3,6,24,128]{4,3,2,1,0:T(8,128)(2,1)} slice(bf16[1,7,13,49,128]{4,3,2,1,0:T(8,128)(2,1)S(1)} %fusion.3), slice={[0:1:1], [2:7:2], [2:13:2], [1:49:2], [0:128:1]} | slice | bytes 221184 | tf_op jit(solution)/shard_map/slice | solution.py:14
  212.5 5.5 %slice.309 = bf16[1,3,6,24,128]{4,3,2,1,0:T(8,128)(2,1)} slice(bf16[1,7,13,49,128]{4,3,2,1,0:T(8,128)(2,1)S(1)} %fusion.3), slice={[0:1:1], [2:7:2], [2:13:2], [2:49:2], [0:128:1]} | slice | bytes 221184 | tf_op jit(solution)/shard_map/slice | solution.py:14
  270.4 8.4 %all-to-all-start = ((bf16[8,2,6912]{2,1,0:T(2,128)(2,1)}), bf16[8,2,6912]{2,1,0:T(2,128)(2,1)S(1)}, u32[]{:S(2)}, u32[]{:S(2)}) async-start(bf16[8,2,6912]{2,1,0:T(2,128)(2,1)} %reshape.371), calls=%async_computation | async-start | bytes 442368 | tf_op jit(solution)/shard_map/all_to_all | solution.py:92
  293.3 6.5 %all-to-all-start.1 = ((bf16[8,2,6912]{2,1,0:T(2,128)(2,1)}), bf16[8,2,6912]{2,1,0:T(2,128)(2,1)S(1)}, u32[]{:S(2)}, u32[]{:S(2)}) async-start(bf16[8,2,6912]{2,1,0:T(2,128)(2,1)} %reshape.373), calls=%async_computation.1 | async-start | bytes 442368 | tf_op jit(solution)/shard_map/all_to_all | solution.py:94
  305.2 5.6 %all-to-all-done.1 = bf16[8,2,6912]{2,1,0:T(2,128)(2,1)S(1)} async-done(((bf16[8,2,6912]{2,1,0:T(2,128)(2,1)}), bf16[8,2,6912]{2,1,0:T(2,128)(2,1)S(1)}, u32[]{:S(2)}, u32[]{:S(2)}) %all-to-all-start.1) | async-done | bytes 221216 | tf_op jit(solution)/shard_map/all_to_all | solution.py:94
  323.0 62.4 %reduce-scatter.5.cloned.1.call-done = f32[3,3,3,128,8]{3,4,2,1,0:T(8,128)} async-done(((f32[3,3,3,128,256]{3,4,2,1,0:T(8,128)}), f32[3,3,3,128,8]{3,4,2,1,0:T(8,128)}) %reduce-scatter.5.cloned.1.call-update) | async-done | bytes 110608 | tf_op jit(solution)/shard_map/reduce_scatter | solution.py:139
  397.9 74.8 %reduce-scatter.7.cloned.1.call-done = f32[16,216]{1,0:T(8,128)} async-done(((f32[128,216]{1,0:T(8,128)}), f32[16,216]{1,0:T(8,128)}) %reduce-scatter.7.cloned.1.call-update) | async-done | bytes 13840
  (283 shorter events, 159.3 us)
Async XLA Ops:
  13.1 21.9 %all-to-all-start.3 = ((bf16[8,2,6912]{2,1,0:T(2,128)(2,1)}), bf16[8,2,6912]{2,1,0:T(2,128)(2,1)S(1)}, u32[]{:S(2)}, u32[]{:S(2)}) async-start(bf16[8,2,6912]{2,1,0:T(2,128)(2,1)} %reshape.377), calls=%async_computation.3 | async-start | bytes 442368 | tf_op jit(solution)/shard_map/all_to_all | solution.py:114
  24.9 19.2 %collective-permute-start = (bf16[1,1,12,48,128]{4,3,2,1,0:T(8,128)(2,1)S(1)}, bf16[1,1,12,48,128]{4,3,2,1,0:T(8,128)(2,1)S(1)}, u32[]{:S(2)}, u32[]{:S(2)}) collective-permute-start(bf16[1,1,12,48,128]{4,3,2,1,0:T(8,128)(2,1)S(1)} %slice.255), channel_id=1, source_target_pairs={{0,32},{32,64},{64,96},{96,128},{128,160},{160,192},{192,224},{1,3... | collective-permute-start | bytes 442376 | tf_op jit(solution)/shard_map/ppermute | solution.py:10
  37.0 7.2 %copy-start.5 = (bf16[1,6,12,48,128]{4,3,2,1,0:T(8,128)(2,1)S(1)}, bf16[1,6,12,48,128]{4,3,2,1,0:T(8,128)(2,1)}, u32[]{:S(2)}) copy-start(bf16[1,6,12,48,128]{4,3,2,1,0:T(8,128)(2,1)} %param.3) | copy-start | bytes 2654212
  39.2 11.3 %all-to-all-start.4 = ((bf16[4,2,13824]{2,1,0:T(2,128)(2,1)}), bf16[4,2,13824]{2,1,0:T(2,128)(2,1)S(1)}, u32[]{:S(2)}, u32[]{:S(2)}) async-start(bf16[4,2,13824]{2,1,0:T(2,128)(2,1)} %reshape.379), calls=%async_computation.4 | async-start | bytes 442368 | tf_op jit(solution)/shard_map/all_to_all | solution.py:113
  44.9 59.2 %collective-permute-start.1 = (bf16[1,7,1,48,128]{4,3,2,1,0:T(8,128)(2,1)}, bf16[1,7,1,48,128]{4,3,2,1,0:T(8,128)(2,1)S(1)}, u32[]{:S(2)}, u32[]{:S(2)}) collective-permute-start(bf16[1,7,1,48,128]{4,3,2,1,0:T(8,128)(2,1)} %slice.318), channel_id=1, source_target_pairs={{0,8},{8,16},{16,24},{1,9},{9,17},{17,25},{2,10},{10,18},{18,26},{... | collective-permute-start | bytes 258056 | tf_op jit(solution)/shard_map/ppermute | solution.py:10
  52.2 7.5 %copy-start.50 = (bf16[3,3,3,16,8]{3,4,2,1,0:T(8,128)(2,1)S(1)}, bf16[3,3,3,16,8]{3,4,2,1,0:T(8,128)(2,1)}, u32[]{:S(2)}) copy-start(bf16[3,3,3,16,8]{3,4,2,1,0:T(8,128)(2,1)} %param.4) | copy-start | bytes 20740
  54.8 163.3 %all-to-all-start.5 = ((bf16[8,2,6912]{2,1,0:T(2,128)(2,1)}), bf16[8,2,6912]{2,1,0:T(2,128)(2,1)S(1)}, u32[]{:S(2)}, u32[]{:S(2)}) async-start(bf16[8,2,6912]{2,1,0:T(2,128)(2,1)} %reshape.381), calls=%async_computation.5 | async-start | bytes 442368 | tf_op jit(solution)/shard_map/all_to_all | solution.py:120
  59.7 178.3 %all-gather.2.cloned.1.call-start = ((), (), s32[]{:S(2)}) async-start(), calls=%async_computation.8 | async-start | bytes 1990656 | tf_op jit(solution)/shard_map/all_gather | solution.py:70
  103.8 281.5 %reduce-scatter.5.cloned.1.call-start = ((), (), s32[]{:S(2)}) async-start(), calls=%async_computation.9 | async-start | bytes 3649536 | tf_op jit(solution)/shard_map/reduce_scatter | solution.py:139
  112.1 112.6 %copy-start.8 = (bf16[1,3,6,24,128]{4,3,2,1,0:T(8,128)(2,1)}, bf16[1,3,6,24,128]{4,3,2,1,0:T(8,128)(2,1)S(1)}, u32[]{:S(2)}) copy-start(bf16[1,3,6,24,128]{4,3,2,1,0:T(8,128)(2,1)S(1)} %slice.265) | copy-start | bytes 331780
  195.4 33.9 %copy-start.6 = (bf16[1,3,6,24,128]{4,3,2,1,0:T(8,128)(2,1)}, bf16[1,3,6,24,128]{4,3,2,1,0:T(8,128)(2,1)S(1)}, u32[]{:S(2)}) copy-start(bf16[1,3,6,24,128]{4,3,2,1,0:T(8,128)(2,1)S(1)} %slice.299) | copy-start | bytes 331780
  195.9 33.7 %copy-start.10 = (bf16[1,3,6,24,128]{4,3,2,1,0:T(8,128)(2,1)}, bf16[1,3,6,24,128]{4,3,2,1,0:T(8,128)(2,1)S(1)}, u32[]{:S(2)}) copy-start(bf16[1,3,6,24,128]{4,3,2,1,0:T(8,128)(2,1)S(1)} %slice.301) | copy-start | bytes 331780
  219.8 3.8 copy-start.48
  221.4 3.5 copy-start.12
  224.1 1.8 copy-start.27
  238.0 2.7 copy-start.1
  257.1 1.9 copy-start.34
  266.7 12.0 %copy-start.2 = (f32[1,4,7,2,50,128]{5,1,4,3,2,0:T(4,128)S(1)}, f32[1,4,7,2,50,128]{5,1,4,3,2,0:T(4,128)}, u32[]{:S(2)}) copy-start(f32[1,4,7,2,50,128]{5,1,4,3,2,0:T(4,128)} %copy.225) | copy-start | bytes 4300804
  270.4 14.1 %all-to-all-start = ((bf16[8,2,6912]{2,1,0:T(2,128)(2,1)}), bf16[8,2,6912]{2,1,0:T(2,128)(2,1)S(1)}, u32[]{:S(2)}, u32[]{:S(2)}) async-start(bf16[8,2,6912]{2,1,0:T(2,128)(2,1)} %reshape.371), calls=%async_computation | async-start | bytes 442368 | tf_op jit(solution)/shard_map/all_to_all | solution.py:92
  281.0 18.8 %collective-permute-start.2 = (f32[1,1,13,49,128]{4,1,3,2,0:T(1,128)S(1)}, f32[1,1,13,49,128]{4,1,3,2,0:T(1,128)S(1)}, u32[]{:S(2)}, u32[]{:S(2)}) collective-permute-start(f32[1,1,13,49,128]{4,1,3,2,0:T(1,128)S(1)} %slice.348), channel_id=1, source_target_pairs={{32,0},{64,32},{96,64},{128,96},{160,128},{192,160},{224,192},{33,... | collective-permute-start | bytes 978440 | tf_op jit(solution)/shard_map/ppermute | solution.py:10
  293.3 17.4 %all-to-all-start.1 = ((bf16[8,2,6912]{2,1,0:T(2,128)(2,1)}), bf16[8,2,6912]{2,1,0:T(2,128)(2,1)S(1)}, u32[]{:S(2)}, u32[]{:S(2)}) async-start(bf16[8,2,6912]{2,1,0:T(2,128)(2,1)} %reshape.373), calls=%async_computation.1 | async-start | bytes 442368 | tf_op jit(solution)/shard_map/all_to_all | solution.py:94
  303.7 88.3 %collective-permute-start.3 = (bf16[1,6,1,49,128]{4,1,3,2,0:T(8,128)(2,1)S(1)}, bf16[1,6,1,49,128]{4,1,3,2,0:T(8,128)(2,1)S(1)}, u32[]{:S(2)}, u32[]{:S(2)}) collective-permute-start(bf16[1,6,1,49,128]{4,1,3,2,0:T(8,128)(2,1)S(1)} %slice.352), channel_id=1, source_target_pairs={{8,0},{16,8},{24,16},{9,1},{17,9},{25,17},{10,2},{18,10},{26,18},{... | collective-permute-start | bytes 225800 | tf_op jit(solution)/shard_map/ppermute | solution.py:10
  319.5 75.0 %all-to-all-start.2 = ((bf16[4,2,13824]{2,1,0:T(2,128)(2,1)}), bf16[4,2,13824]{2,1,0:T(2,128)(2,1)S(1)}, u32[]{:S(2)}, u32[]{:S(2)}) async-start(bf16[4,2,13824]{2,1,0:T(2,128)(2,1)} %reshape.375), calls=%async_computation.2 | async-start | bytes 442368 | tf_op jit(solution)/shard_map/all_to_all | solution.py:93
  322.9 149.8 %reduce-scatter.7.cloned.1.call-start = ((), (), s32[]{:S(2)}) async-start(), calls=%async_computation.10 | async-start | bytes 147456
  (41 other events, 58.0 us)
Sparse Core Ops, SparseCore 0:
  104.0 68.6 all-gather.1
  392.1 80.5 reduce-scatter.6
Sparse Core Ops, SparseCore 1:
  238.1 147.2 reduce-scatter.4
where the time goes:
time: 491 us; the launch traced here: 482 us
  local copies, waits for them, and re-layouts  187 us (38%)
  waiting for transfers between devices  152 us (31%)
  starting transfers between devices  49.8 us (10%)
  blocking collectives  42.8 us (9%)
  matrix products  26.6 us (5%)
  between operations  17.2 us (4%)
  other arithmetic  5.71 us (1%)
    slice x27, local copies, waits for them, and re-layouts, strided_patch(): extended[:, tap_d:tap_d + 2 * depth:2, tap_h:tap_h + 2 * height:2, tap_w:...  113 us
    unnamed x4, waiting for transfers between devices  74.9 us
    reduce_scatter x1, waiting for transfers between devices, on_device(): lax.psum_scatter(kernel_terms, ('sy', 'af'), scatter_dimension=4, tiled=T...  62.4 us
    unnamed x122, local copies, waits for them, and re-layouts  47.6 us
    all_gather x1, blocking collectives, on_device(): kernel_part = lax.all_gather(kernel, ('sy', 'af'), axis=4, tiled=True)  42.8 us
    dot_general x27, matrix products, spread_back(): lax.dot_general(grad_flat, kernel_full[tap_d, tap_h, tap_w], (((1,), (1,)...  14.2 us
    all_to_all x1, starting transfers between devices, on_device(): lax.all_to_all(grad_after, 'sx', split_axis=1, concat_axis=0, tiled=True)  10.9 us
    ppermute x4, starting transfers between devices, from_behind(): lax.ppermute(value, axis, [(source, source + steps) for source in range(l...  10.6 us
  transfers between devices with their start and end apart: 13, of which 6 were waited for; matrix products, arithmetic and copies ran while one was open for 43% of the time, Pallas kernels for 0%

commit v1 on v0

--- a/solution.py
+++ b/solution.py
@@ -67,7 +67,9 @@
     n_sy = lax.axis_size("sy")
     n_af = lax.axis_size("af")
     kernel_part = lax.all_gather(kernel, ("sy", "af"), axis=4, tiled=True)
-    kernel_full = lax.all_gather(kernel_part, "sx", axis=3, tiled=True)
+    kernel_full = jnp.concatenate(
+        lax.all_to_all(jnp.stack([kernel_part] * lax.axis_size("sx")), "sx", 0, 0), axis=3
+    )
     filters = kernel_full.shape[4]
     per_dev = filters // (n_sy * n_af)
     below = from_behind(volume[:, -1:], "sx", 1)

time: 491 us -> 504 us (1.026)
  starting transfers between devices: 49.8 us -> 57.9 us
  waiting for transfers between devices: 152 us -> 159 us
    all_to_all x0 -> x1, waiting for transfers between devices: none -> 17.4 us  [on_device(): lax.all_to_all(jnp.stack([kernel_part] * lax.axis_size('sx')), 'sx', 0, 0)]
    reduce_scatter x1, waiting for transfers between devices: 62.4 us -> 48.7 us  [on_device(): lax.psum_scatter(kernel_terms, ('sy', 'af'), scatter_dimension=4, tiled=T...]
    unnamed x4 -> x3, waiting for transfers between devices: 74.9 us -> 76.5 us
    unnamed x122 -> x120, local copies, waits for them, and re-layouts: 47.6 us -> 47.2 us
  transfers between devices with their start and end apart: 13 -> 13, of which waited for: 6 -> 7; matrix products, arithmetic and copies ran while one was open for 43% -> 42% of each run, Pallas kernels for 0% -> 0%
where the time goes in v1:
time: 504 us; the launch traced here: 495 us
  local copies, waits for them, and re-layouts  190 us (38%)
  waiting for transfers between devices  159 us (32%)
  starting transfers between devices  57.9 us (11%)
  blocking collectives  42.9 us (9%)
  matrix products  24.8 us (5%)
  between operations  15.8 us (3%)
  other arithmetic  5.66 us (1%)
    slice x27, local copies, waits for them, and re-layouts, strided_patch(): extended[:, tap_d:tap_d + 2 * depth:2, tap_h:tap_h + 2 * height:2, tap_w:...  113 us
    unnamed x3, waiting for transfers between devices  76.5 us
    reduce_scatter x1, waiting for transfers between devices, on_device(): lax.psum_scatter(kernel_terms, ('sy', 'af'), scatter_dimension=4, tiled=T...  48.7 us
    unnamed x120, local copies, waits for them, and re-layouts  47.2 us
    all_gather x1, blocking collectives, on_device(): kernel_part = lax.all_gather(kernel, ('sy', 'af'), axis=4, tiled=True)  42.9 us
    all_to_all x1, waiting for transfers between devices, on_device(): lax.all_to_all(jnp.stack([kernel_part] * lax.axis_size('sx')), 'sx', 0, 0)  17.4 us
    dot_general x27, matrix products, spread_back(): lax.dot_general(grad_flat, kernel_full[tap_d, tap_h, tap_w], (((1,), (1,)...  12.4 us
    all_to_all x1, starting transfers between devices, on_device(): lax.all_to_all(grad_after, 'sx', split_axis=1, concat_axis=0, tiled=True)  10.9 us
  transfers between devices with their start and end apart: 13, of which 7 were waited for; matrix products, arithmetic and copies ran while one was open for 42% of the time, Pallas kernels for 0%

profile of v1, /device:TPU:8, one launch (start us, length us, event | category | flops | bytes accessed | tf_op | source)
XLA Modules:
  0.0 495.2 jit_solution(3185033382749448338)
XLA Ops:
  12.2 10.9 %all-to-all-start.4 = ((bf16[8,2,6912]{2,1,0:T(2,128)(2,1)}), bf16[8,2,6912]{2,1,0:T(2,128)(2,1)S(1)}, u32[]{:S(2)}, u32[]{:S(2)}) async-start(bf16[8,2,6912]{2,1,0:T(2,128)(2,1)} %reshape.387), calls=%async_computation.4 | async-start | bytes 442368 | tf_op jit(solution)/shard_map/all_to_all | solution.py:116
  28.0 6.1 %all-to-all-done.4 = bf16[8,2,6912]{2,1,0:T(2,128)(2,1)S(1)} async-done(((bf16[8,2,6912]{2,1,0:T(2,128)(2,1)}), bf16[8,2,6912]{2,1,0:T(2,128)(2,1)S(1)}, u32[]{:S(2)}, u32[]{:S(2)}) %all-to-all-start.4) | async-done | bytes 221216 | tf_op jit(solution)/shard_map/all_to_all | solution.py:116
  58.9 42.9 %all_gather.3 = bf16[3,3,3,16,256]{3,4,2,1,0:T(8,128)(2,1)S(1)} all-gather(bf16[3,3,3,16,8]{3,4,2,1,0:T(8,128)(2,1)S(1)} %copy-done.49), channel_id=1, replica_groups=mesh['sx'=8,'sy'=4,'af'=8] {'sy','af'}, dimensions={4}, use_global_device_ids=true | all-gather | bytes 228096 | tf_op jit(solution)/shard_map/all_gather | solution.py:69
  103.0 5.5 %slice.257 = bf16[1,3,6,24,128]{4,3,2,1,0:T(8,128)(2,1)} slice(bf16[1,7,13,49,128]{4,3,2,1,0:T(8,128)(2,1)S(1)} %fusion.3), slice={[0:1:1], [0:6:2], [0:12:2], [0:48:2], [0:128:1]} | slice | bytes 221184 | tf_op jit(solution)/shard_map/slice | solution.py:14
  110.5 5.5 %slice.267 = bf16[1,3,6,24,128]{4,3,2,1,0:T(8,128)(2,1)} slice(bf16[1,7,13,49,128]{4,3,2,1,0:T(8,128)(2,1)S(1)} %fusion.3), slice={[0:1:1], [0:6:2], [1:13:2], [2:49:2], [0:128:1]} | slice | bytes 221184 | tf_op jit(solution)/shard_map/slice | solution.py:14
  116.0 5.5 %slice.269 = bf16[1,3,6,24,128]{4,3,2,1,0:T(8,128)(2,1)} slice(bf16[1,7,13,49,128]{4,3,2,1,0:T(8,128)(2,1)S(1)} %fusion.3), slice={[0:1:1], [0:6:2], [2:13:2], [0:48:2], [0:128:1]} | slice | bytes 221184 | tf_op jit(solution)/shard_map/slice | solution.py:14
  121.5 5.5 %slice.271 = bf16[1,3,6,24,128]{4,3,2,1,0:T(8,128)(2,1)} slice(bf16[1,7,13,49,128]{4,3,2,1,0:T(8,128)(2,1)S(1)} %fusion.3), slice={[0:1:1], [0:6:2], [2:13:2], [1:49:2], [0:128:1]} | slice | bytes 221184 | tf_op jit(solution)/shard_map/slice | solution.py:14
  127.0 5.6 %slice.273 = bf16[1,3,6,24,128]{4,3,2,1,0:T(8,128)(2,1)} slice(bf16[1,7,13,49,128]{4,3,2,1,0:T(8,128)(2,1)S(1)} %fusion.3), slice={[0:1:1], [0:6:2], [2:13:2], [2:49:2], [0:128:1]} | slice | bytes 221184 | tf_op jit(solution)/shard_map/slice | solution.py:14
  143.5 5.5 %slice.279 = bf16[1,3,6,24,128]{4,3,2,1,0:T(8,128)(2,1)} slice(bf16[1,7,13,49,128]{4,3,2,1,0:T(8,128)(2,1)S(1)} %fusion.3), slice={[0:1:1], [1:7:2], [0:12:2], [2:49:2], [0:128:1]} | slice | bytes 221184 | tf_op jit(solution)/shard_map/slice | solution.py:14
  159.9 5.5 %slice.285 = bf16[1,3,6,24,128]{4,3,2,1,0:T(8,128)(2,1)} slice(bf16[1,7,13,49,128]{4,3,2,1,0:T(8,128)(2,1)S(1)} %fusion.3), slice={[0:1:1], [1:7:2], [1:13:2], [2:49:2], [0:128:1]} | slice | bytes 221184 | tf_op jit(solution)/shard_map/slice | solution.py:14
  165.4 5.5 %slice.287 = bf16[1,3,6,24,128]{4,3,2,1,0:T(8,128)(2,1)} slice(bf16[1,7,13,49,128]{4,3,2,1,0:T(8,128)(2,1)S(1)} %fusion.3), slice={[0:1:1], [1:7:2], [2:13:2], [0:48:2], [0:128:1]} | slice | bytes 221184 | tf_op jit(solution)/shard_map/slice | solution.py:14
  170.9 5.5 %slice.289 = bf16[1,3,6,24,128]{4,3,2,1,0:T(8,128)(2,1)} slice(bf16[1,7,13,49,128]{4,3,2,1,0:T(8,128)(2,1)S(1)} %fusion.3), slice={[0:1:1], [1:7:2], [2:13:2], [1:49:2], [0:128:1]} | slice | bytes 221184 | tf_op jit(solution)/shard_map/slice | solution.py:14
  176.5 5.5 %slice.291 = bf16[1,3,6,24,128]{4,3,2,1,0:T(8,128)(2,1)} slice(bf16[1,7,13,49,128]{4,3,2,1,0:T(8,128)(2,1)S(1)} %fusion.3), slice={[0:1:1], [1:7:2], [2:13:2], [2:49:2], [0:128:1]} | slice | bytes 221184 | tf_op jit(solution)/shard_map/slice | solution.py:14
  194.5 5.5 %slice.303 = bf16[1,3,6,24,128]{4,3,2,1,0:T(8,128)(2,1)} slice(bf16[1,7,13,49,128]{4,3,2,1,0:T(8,128)(2,1)S(1)} %fusion.3), slice={[0:1:1], [2:7:2], [1:13:2], [2:49:2], [0:128:1]} | slice | bytes 221184 | tf_op jit(solution)/shard_map/slice | solution.py:14
  200.0 5.5 %slice.305 = bf16[1,3,6,24,128]{4,3,2,1,0:T(8,128)(2,1)} slice(bf16[1,7,13,49,128]{4,3,2,1,0:T(8,128)(2,1)S(1)} %fusion.3), slice={[0:1:1], [2:7:2], [2:13:2], [0:48:2], [0:128:1]} | slice | bytes 221184 | tf_op jit(solution)/shard_map/slice | solution.py:14
  205.5 5.5 %slice.307 = bf16[1,3,6,24,128]{4,3,2,1,0:T(8,128)(2,1)} slice(bf16[1,7,13,49,128]{4,3,2,1,0:T(8,128)(2,1)S(1)} %fusion.3), slice={[0:1:1], [2:7:2], [2:13:2], [1:49:2], [0:128:1]} | slice | bytes 221184 | tf_op jit(solution)/shard_map/slice | solution.py:14
  211.0 5.6 %slice.309 = bf16[1,3,6,24,128]{4,3,2,1,0:T(8,128)(2,1)} slice(bf16[1,7,13,49,128]{4,3,2,1,0:T(8,128)(2,1)S(1)} %fusion.3), slice={[0:1:1], [2:7:2], [2:13:2], [2:49:2], [0:128:1]} | slice | bytes 221184 | tf_op jit(solution)/shard_map/slice | solution.py:14
  242.3 17.4 %all-to-all-done = bf16[8,3,3,3,16,256]{5,4,3,2,1,0:T(8,128)(2,1)} async-done(((bf16[8,3,3,3,16,256]{5,4,3,2,1,0:T(8,128)(2,1)}), bf16[8,3,3,3,16,256]{5,4,3,2,1,0:T(8,128)(2,1)}, u32[]{:S(2)}, u32[]{:S(2)}) %all-to-all-start) | async-done | bytes 1769504 | tf_op jit(solution)/shard_map/all_to_all | solution.py:71
  291.5 6.4 %all-to-all-start.1 = ((bf16[8,2,6912]{2,1,0:T(2,128)(2,1)}), bf16[8,2,6912]{2,1,0:T(2,128)(2,1)S(1)}, u32[]{:S(2)}, u32[]{:S(2)}) async-start(bf16[8,2,6912]{2,1,0:T(2,128)(2,1)} %reshape.381), calls=%async_computation.1 | async-start | bytes 442368 | tf_op jit(solution)/shard_map/all_to_all | solution.py:94
  313.1 10.2 %all-to-all-start.2 = ((bf16[8,2,6912]{2,1,0:T(2,128)(2,1)}), bf16[8,2,6912]{2,1,0:T(2,128)(2,1)S(1)}, u32[]{:S(2)}, u32[]{:S(2)}) async-start(bf16[8,2,6912]{2,1,0:T(2,128)(2,1)} %reshape.383), calls=%async_computation.2 | async-start | bytes 442368 | tf_op jit(solution)/shard_map/all_to_all | solution.py:96
  328.6 5.7 %all-to-all-done.2 = bf16[8,2,6912]{2,1,0:T(2,128)(2,1)S(1)} async-done(((bf16[8,2,6912]{2,1,0:T(2,128)(2,1)}), bf16[8,2,6912]{2,1,0:T(2,128)(2,1)S(1)}, u32[]{:S(2)}, u32[]{:S(2)}) %all-to-all-start.2) | async-done | bytes 221216 | tf_op jit(solution)/shard_map/all_to_all | solution.py:96
  343.0 5.7 %all-to-all-start.3 = ((bf16[4,2,13824]{2,1,0:T(2,128)(2,1)}), bf16[4,2,13824]{2,1,0:T(2,128)(2,1)S(1)}, u32[]{:S(2)}, u32[]{:S(2)}) async-start(bf16[4,2,13824]{2,1,0:T(2,128)(2,1)} %reshape.385), calls=%async_computation.3 | async-start | bytes 442368 | tf_op jit(solution)/shard_map/all_to_all | solution.py:95
  348.7 48.7 %reduce-scatter.5.cloned.1.call-done = f32[3,3,3,128,8]{3,4,2,1,0:T(8,128)} async-done(((f32[3,3,3,128,256]{3,4,2,1,0:T(8,128)}), f32[3,3,3,128,8]{3,4,2,1,0:T(8,128)}) %reduce-scatter.5.cloned.1.call-update) | async-done | bytes 110608 | tf_op jit(solution)/shard_map/reduce_scatter | solution.py:141
  410.1 76.5 %reduce-scatter.7.cloned.1.call-done = f32[16,216]{1,0:T(8,128)} async-done(((f32[128,216]{1,0:T(8,128)}), f32[16,216]{1,0:T(8,128)}) %reduce-scatter.7.cloned.1.call-update) | async-done | bytes 13840
  (282 shorter events, 171.6 us)
Async XLA Ops:
  12.2 21.9 %all-to-all-start.4 = ((bf16[8,2,6912]{2,1,0:T(2,128)(2,1)}), bf16[8,2,6912]{2,1,0:T(2,128)(2,1)S(1)}, u32[]{:S(2)}, u32[]{:S(2)}) async-start(bf16[8,2,6912]{2,1,0:T(2,128)(2,1)} %reshape.387), calls=%async_computation.4 | async-start | bytes 442368 | tf_op jit(solution)/shard_map/all_to_all | solution.py:116
  24.1 19.2 %collective-permute-start = (bf16[1,1,12,48,128]{4,3,2,1,0:T(8,128)(2,1)S(1)}, bf16[1,1,12,48,128]{4,3,2,1,0:T(8,128)(2,1)S(1)}, u32[]{:S(2)}, u32[]{:S(2)}) collective-permute-start(bf16[1,1,12,48,128]{4,3,2,1,0:T(8,128)(2,1)S(1)} %slice.255), channel_id=1, source_target_pairs={{0,32},{32,64},{64,96},{96,128},{128,160},{160,192},{192,224},{1,3... | collective-permute-start | bytes 442376 | tf_op jit(solution)/shard_map/ppermute | solution.py:10
  36.1 7.2 %copy-start.4 = (bf16[1,6,12,48,128]{4,3,2,1,0:T(8,128)(2,1)S(1)}, bf16[1,6,12,48,128]{4,3,2,1,0:T(8,128)(2,1)}, u32[]{:S(2)}) copy-start(bf16[1,6,12,48,128]{4,3,2,1,0:T(8,128)(2,1)} %param.3) | copy-start | bytes 2654212
  38.4 11.3 %all-to-all-start.5 = ((bf16[4,2,13824]{2,1,0:T(2,128)(2,1)}), bf16[4,2,13824]{2,1,0:T(2,128)(2,1)S(1)}, u32[]{:S(2)}, u32[]{:S(2)}) async-start(bf16[4,2,13824]{2,1,0:T(2,128)(2,1)} %reshape.389), calls=%async_computation.5 | async-start | bytes 442368 | tf_op jit(solution)/shard_map/all_to_all | solution.py:115
  44.1 58.5 %collective-permute-start.1 = (bf16[1,7,1,48,128]{4,3,2,1,0:T(8,128)(2,1)}, bf16[1,7,1,48,128]{4,3,2,1,0:T(8,128)(2,1)S(1)}, u32[]{:S(2)}, u32[]{:S(2)}) collective-permute-start(bf16[1,7,1,48,128]{4,3,2,1,0:T(8,128)(2,1)} %slice.318), channel_id=1, source_target_pairs={{0,8},{8,16},{16,24},{1,9},{9,17},{17,25},{2,10},{10,18},{18,26},{... | collective-permute-start | bytes 258056 | tf_op jit(solution)/shard_map/ppermute | solution.py:10
  51.4 7.5 %copy-start.49 = (bf16[3,3,3,16,8]{3,4,2,1,0:T(8,128)(2,1)S(1)}, bf16[3,3,3,16,8]{3,4,2,1,0:T(8,128)(2,1)}, u32[]{:S(2)}) copy-start(bf16[3,3,3,16,8]{3,4,2,1,0:T(8,128)(2,1)} %param.4) | copy-start | bytes 20740
  53.9 162.6 %all-to-all-start.6 = ((bf16[8,2,6912]{2,1,0:T(2,128)(2,1)}), bf16[8,2,6912]{2,1,0:T(2,128)(2,1)S(1)}, u32[]{:S(2)}, u32[]{:S(2)}) async-start(bf16[8,2,6912]{2,1,0:T(2,128)(2,1)} %reshape.391), calls=%async_computation.6 | async-start | bytes 442368 | tf_op jit(solution)/shard_map/all_to_all | solution.py:122
  110.5 118.4 %copy-start.7 = (bf16[1,3,6,24,128]{4,3,2,1,0:T(8,128)(2,1)}, bf16[1,3,6,24,128]{4,3,2,1,0:T(8,128)(2,1)S(1)}, u32[]{:S(2)}) copy-start(bf16[1,3,6,24,128]{4,3,2,1,0:T(8,128)(2,1)S(1)} %slice.265) | copy-start | bytes 331780
  193.9 39.7 %copy-start.5 = (bf16[1,3,6,24,128]{4,3,2,1,0:T(8,128)(2,1)}, bf16[1,3,6,24,128]{4,3,2,1,0:T(8,128)(2,1)S(1)}, u32[]{:S(2)}) copy-start(bf16[1,3,6,24,128]{4,3,2,1,0:T(8,128)(2,1)S(1)} %slice.299) | copy-start | bytes 331780
  194.5 39.4 %copy-start.9 = (bf16[1,3,6,24,128]{4,3,2,1,0:T(8,128)(2,1)}, bf16[1,3,6,24,128]{4,3,2,1,0:T(8,128)(2,1)S(1)}, u32[]{:S(2)}) copy-start(bf16[1,3,6,24,128]{4,3,2,1,0:T(8,128)(2,1)S(1)} %slice.301) | copy-start | bytes 331780
  217.9 41.8 %all-to-all-start = ((bf16[8,3,3,3,16,256]{5,4,3,2,1,0:T(8,128)(2,1)}), bf16[8,3,3,3,16,256]{5,4,3,2,1,0:T(8,128)(2,1)}, u32[]{:S(2)}, u32[]{:S(2)}) async-start(bf16[8,3,3,3,16,256]{5,4,3,2,1,0:T(8,128)(2,1)} %stack.140), calls=%async_computation | async-start | bytes 3538944 | tf_op jit(solution)/shard_map/all_to_all | solution.py:71
  222.2 175.2 %reduce-scatter.5.cloned.1.call-start = ((), (), s32[]{:S(2)}) async-start(), calls=%async_computation.9 | async-start | bytes 3649536 | tf_op jit(solution)/shard_map/reduce_scatter | solution.py:141
  224.0 3.9 copy-start.47
  225.7 3.5 copy-start.11
  227.9 1.8 copy-start.18
  228.4 1.8 copy-start.26
  278.3 1.9 copy-start.33
  287.9 10.1 %copy-start.1 = (f32[1,4,7,2,50,128]{5,1,4,3,2,0:T(4,128)S(1)}, f32[1,4,7,2,50,128]{5,1,4,3,2,0:T(4,128)}, u32[]{:S(2)}) copy-start(f32[1,4,7,2,50,128]{5,1,4,3,2,0:T(4,128)} %copy.227) | copy-start | bytes 4300804
  291.5 12.7 %all-to-all-start.1 = ((bf16[8,2,6912]{2,1,0:T(2,128)(2,1)}), bf16[8,2,6912]{2,1,0:T(2,128)(2,1)S(1)}, u32[]{:S(2)}, u32[]{:S(2)}) async-start(bf16[8,2,6912]{2,1,0:T(2,128)(2,1)} %reshape.381), calls=%async_computation.1 | async-start | bytes 442368 | tf_op jit(solution)/shard_map/all_to_all | solution.py:94
  300.3 23.1 %collective-permute-start.2 = (f32[1,1,13,49,128]{4,1,3,2,0:T(1,128)S(1)}, f32[1,1,13,49,128]{4,1,3,2,0:T(1,128)S(1)}, u32[]{:S(2)}, u32[]{:S(2)}) collective-permute-start(f32[1,1,13,49,128]{4,1,3,2,0:T(1,128)S(1)} %slice.348), channel_id=1, source_target_pairs={{32,0},{64,32},{96,64},{128,96},{160,128},{192,160},{224,192},{33,... | collective-permute-start | bytes 978440 | tf_op jit(solution)/shard_map/ppermute | solution.py:10
  313.1 21.2 %all-to-all-start.2 = ((bf16[8,2,6912]{2,1,0:T(2,128)(2,1)}), bf16[8,2,6912]{2,1,0:T(2,128)(2,1)S(1)}, u32[]{:S(2)}, u32[]{:S(2)}) async-start(bf16[8,2,6912]{2,1,0:T(2,128)(2,1)} %reshape.383), calls=%async_computation.2 | async-start | bytes 442368 | tf_op jit(solution)/shard_map/all_to_all | solution.py:96
  327.3 76.8 %collective-permute-start.3 = (bf16[1,6,1,49,128]{4,1,3,2,0:T(8,128)(2,1)S(1)}, bf16[1,6,1,49,128]{4,1,3,2,0:T(8,128)(2,1)S(1)}, u32[]{:S(2)}, u32[]{:S(2)}) collective-permute-start(bf16[1,6,1,49,128]{4,1,3,2,0:T(8,128)(2,1)S(1)} %slice.352), channel_id=1, source_target_pairs={{8,0},{16,8},{24,16},{9,1},{17,9},{25,17},{10,2},{18,10},{26,18},{... | collective-permute-start | bytes 225800 | tf_op jit(solution)/shard_map/ppermute | solution.py:10
  343.0 63.6 %all-to-all-start.3 = ((bf16[4,2,13824]{2,1,0:T(2,128)(2,1)}), bf16[4,2,13824]{2,1,0:T(2,128)(2,1)S(1)}, u32[]{:S(2)}, u32[]{:S(2)}) async-start(bf16[4,2,13824]{2,1,0:T(2,128)(2,1)} %reshape.385), calls=%async_computation.3 | async-start | bytes 442368 | tf_op jit(solution)/shard_map/all_to_all | solution.py:95
  348.7 137.8 %reduce-scatter.7.cloned.1.call-start = ((), (), s32[]{:S(2)}) async-start(), calls=%async_computation.10 | async-start | bytes 147456
  (40 other events, 56.4 us)
Sparse Core Ops, SparseCore 0:
  242.4 155.0 reduce-scatter.4
  404.2 82.2 reduce-scatter.6
